TPU v7x, 32 devices: a whole 2x2x4 slice. The times are simulated.
32 devices in a mesh: row: 8 (over z, x), col: 2 (over core), rank: 2 (over y).
Axes of the slice: x: 2, y: 2, z: 4, core: 2. Of those that a mesh axis runs over, the one named last changes fastest.
Arguments:
- tensor: bfloat16 [64, 2048, 2048], P(None, 'row', 'col'), may hold values from -6 to 6
- aux_factor: bfloat16 [64, 256], P(None, 'rank'), may hold values from -0.75 to 0.75
- row_factor: bfloat16 [2048, 256], P(('row', 'col'), 'rank'), may hold values from -0.125 to 0.125
- col_factor: bfloat16 [2048, 256], P(('col', 'row'), 'rank'), may hold values from -0.125 to 0.125
Outputs:
- row_result: float32 [2048, 256], P(('row', 'col'), 'rank')
- aux_result: float32 [64, 256], P('row', 'rank')
All inputs are finite; a program needn't handle non-finite values.
Results may differ from a plain program's by a relative error of at most 0.0003.
Values may be sent and summed in bfloat16 or wider, within the bound.
A program may use at most 128 MiB of HBM per device.

v0:
```python
import jax
import jax.numpy as jnp
from jax import lax
from jax.sharding import PartitionSpec as P


def reduce_inner(inner, aux_factor, row_panel):
    aux_panel = aux_factor.astype(jnp.float32)
    aux_count = inner.shape[0]
    row_total = jnp.zeros((inner.shape[1], inner.shape[2]), jnp.float32)
    pieces = []
    for start in range(0, aux_count, 8):
        block = inner[start : start + 8]
        row_total = row_total + jnp.sum(block * aux_panel[start : start + 8][:, None, :], axis=0)
        pieces.append(jnp.sum(block * row_panel[None, :, :], axis=1))
    return (row_total, jnp.concatenate(pieces, axis=0))


def body(tensor, aux_factor, row_factor, col_factor):
    row_panel = lax.all_gather(row_factor, "col", axis=0, tiled=True).astype(jnp.float32)
    width = aux_factor.shape[1]
    aux_count = tensor.shape[0]
    orbits = tensor.shape[1]
    flat = tensor.reshape(aux_count * orbits, tensor.shape[2])
    columns = lax.all_gather(col_factor, "row", axis=0, tiled=True)
    inner = jnp.dot(flat, columns, preferred_element_type=jnp.float32)
    inner = inner.reshape(aux_count, orbits, width)
    row_total, aux_total = reduce_inner(inner, aux_factor, row_panel)
    row_result = lax.psum_scatter(row_total, "col", scatter_dimension=0, tiled=True)
    scattered = lax.psum_scatter(aux_total, "row", scatter_dimension=0, tiled=True)
    aux_result = lax.psum(scattered, "col")
    return (row_result, aux_result)


def solution(mesh):
    return jax.shard_map(
        body,
        mesh=mesh,
        in_specs=(
            P(None, "row", "col"),
            P(None, "rank"),
            P(("row", "col"), "rank"),
            P(("col", "row"), "rank"),
        ),
        out_specs=(P(("row", "col"), "rank"), P("row", "rank")),
        check_vma=False,
    )
```

profile of v0, /device:TPU:0, one launch (start us, length us, event | category | flops | bytes accessed | tf_op | source)
XLA Modules:
  0.0 115.6 jit_solution(7216242594102125668)
XLA Ops:
  7.2 0.0 reduce-scatter.2.cloned.1.call-start
  7.2 0.8 fusion.1
  8.0 32.8 %all_gather.6 = bf16[1024,128]{1,0:T(8,128)(2,1)S(1)} all-gather(bf16[128,128]{1,0:T(8,128)(2,1)} %param.7), channel_id=1, replica_groups=mesh['row'=8,'col'=2,'rank'=2] {'row'}, dimensions={0}, use_global_device_ids=true | all-gather | bytes 294912 | tf_op jit(solution)/shard_map/all_gather | solution.py:25
  40.8 0.0 copy-start.1
  40.8 0.0 copy-start.2
  40.8 14.9 %fusion.2 = f32[16384,128]{1,0:T(8,128)S(1)} fusion(bf16[16384,1024]{1,0:T(8,128)(2,1)} %bitcast.20, bf16[1024,128]{1,0:T(8,128)(2,1)S(1)} %all_gather.6), kind=kOutput, calls=%fused_computation.28 | convolution fusion | flops 4294967296 | bytes 42205184 | tf_op jit(solution)/shard_map/dot_general | solution.py:26
  55.7 0.0 copy-start
  55.7 3.2 %copy-done = f32[16384,128]{1,0:T(8,128)} copy-done((f32[16384,128]{1,0:T(8,128)}, f32[16384,128]{1,0:T(8,128)S(1)}, u32[]{:S(2)}) %copy-start) | copy-done | bytes 8388632
  58.9 0.6 fusion
  59.5 0.2 multiply_reduce_fusion.14
  59.6 0.2 multiply_reduce_fusion.8
  59.8 0.2 multiply_reduce_fusion.10
  59.9 0.2 multiply_reduce_fusion.12
  60.1 0.7 add_add_fusion
  60.8 0.0 reduce-scatter.2.cloned.1.call-update
  60.8 0.0 copy-done.1
  60.8 1.9 %all_gather.7 = bf16[256,128]{1,0:T(8,128)(2,1)S(1)} all-gather(bf16[128,128]{1,0:T(8,128)(2,1)S(1)} %copy-done.1), channel_id=1, replica_groups=mesh['row'=8,'col'=2,'rank'=2] {'col'}, dimensions={0}, use_global_device_ids=true | all-gather | bytes 98304 | tf_op jit(solution)/shard_map/all_gather | solution.py:20
  62.7 4.6 %multiply_reduce_fusion = (f32[8,128]{1,0:T(8,128)S(1)}, f32[8,128]{1,0:T(8,128)S(1)}, f32[8,128]{1,0:T(8,128)S(1)}, f32[8,128]{1,0:T(8,128)S(1)}, f32[8,128]{1,...) fusion(f32[256,128]{1,0:T(8,128)S(1)} %convert_element_type.7, f32[16384,128]{1,0:T(8,128)} %copy-done), kind=kLoop, calls=%fused_computation | loop fusion | flops 4186112 | bytes 8552448 | tf_op jit(solution)/shard_map/reduce_sum | solution.py:15
  67.4 0.0 copy-done.2
  67.4 0.6 dynamic-slice
  68.6 37.1 %all-reduce = f32[64,128]{1,0:T(8,128)S(1)} all-reduce(f32[64,128]{1,0:T(8,128)S(1)} %constant_dynamic-update-slice_fusion), channel_id=3, replica_groups=mesh['row'=8,'col'=2,'rank'=2] {'row'}, use_global_device_ids=true, to_apply=%region_17.0.clone | all-reduce | flops 8192 | bytes 65536
  105.7 3.0 %psum.7 = f32[8,128]{1,0:T(8,128)} all-reduce(f32[8,128]{1,0:T(8,128)S(1)} %constant_dynamic-slice_fusion), channel_id=1, replica_groups=mesh['row'=8,'col'=2,'rank'=2] {'col'}, use_global_device_ids=true, to_apply=%region_18.0 | all-reduce | flops 1024 | bytes 8192 | tf_op jit(solution)/shard_map/psum | solution.py:31
  108.8 0.0 reduce-scatter.2.cloned.1.call-done
  (10 shorter events, 0.0 us)
Async XLA Ops:
  7.2 101.6 %reduce-scatter.2.cloned.1.call-start = ((), (), s32[]{:S(2)}) async-start(), calls=%async_computation.1 | async-start | bytes 196608 | tf_op jit(solution)/shard_map/reduce_scatter | solution.py:29
  40.8 20.1 %copy-start.1 = (bf16[128,128]{1,0:T(8,128)(2,1)S(1)}, bf16[128,128]{1,0:T(8,128)(2,1)}, u32[]{:S(2)}) copy-start(bf16[128,128]{1,0:T(8,128)(2,1)} %param.6) | copy-start | bytes 98308
  40.8 26.6 %copy-start.2 = (u32[32]{0:T(128)S(1)}, u32[32]{0:T(128)}, u32[]{:S(2)}) copy-start(u32[32]{0:T(128)} %constant.4) | copy-start | bytes 388
  55.7 3.2 %copy-start = (f32[16384,128]{1,0:T(8,128)}, f32[16384,128]{1,0:T(8,128)S(1)}, u32[]{:S(2)}) copy-start(f32[16384,128]{1,0:T(8,128)S(1)} %fusion.2) | copy-start | bytes 25165828
Sparse Core Ops, SparseCore 0:
  61.0 8.5 reduce-scatter.1
where the time goes:
time: 116 us
  blocking collectives  74.7 us (64%)
  matrix products  14.9 us (13%)
  between operations  14.8 us (13%)
  other arithmetic  5.94 us (5%)
  local copies, waits for them, and re-layouts  5.2 us (4%)
    unnamed x1, blocking collectives  37.1 us
    all_gather x1, blocking collectives, body(): columns = lax.all_gather(col_factor, 'row', axis=0, tiled=True)  32.8 us
    dot_general x1, matrix products, body(): inner = jnp.dot(flat, columns, preferred_element_type=jnp.float32)  14.9 us
    reduce_sum x1, other arithmetic, reduce_inner(): pieces.append(jnp.sum(block * row_panel[None, :, :], axis=1))  4.59 us
    unnamed x15, local copies, waits for them, and re-layouts  3.83 us
    psum x1, blocking collectives, body(): aux_result = lax.psum(scattered, 'col')  3.04 us
  transfers between devices with their start and end apart: 1, of which 0 were waited for; matrix products, arithmetic and copies ran while one was open for 5% of the time, Pallas kernels for 0%

commit v1 on v0

--- a/solution.py
+++ b/solution.py
@@ -22,7 +22,9 @@
     aux_count = tensor.shape[0]
     orbits = tensor.shape[1]
     flat = tensor.reshape(aux_count * orbits, tensor.shape[2])
-    columns = lax.all_gather(col_factor, "row", axis=0, tiled=True)
+    columns = jnp.concatenate(
+        lax.all_to_all(jnp.stack([col_factor] * lax.axis_size("row")), "row", 0, 0), axis=0
+    )
     inner = jnp.dot(flat, columns, preferred_element_type=jnp.float32)
     inner = inner.reshape(aux_count, orbits, width)
     row_total, aux_total = reduce_inner(inner, aux_factor, row_panel)

time: 116 us -> 88.4 us (0.76)
  blocking collectives: 74.7 us -> 40.3 us
  starting transfers between devices: 0.04 us -> 7.32 us
  waiting for transfers between devices: 0.02 us -> 4.1 us
  other arithmetic: 5.94 us -> 2.56 us
    all_gather x1 -> x0, blocking collectives: 32.8 us -> none  [body(): columns = lax.all_gather(col_factor, 'row', axis=0, tiled=True)]
    all_to_all x0 -> x1, starting transfers between devices: none -> 7.28 us  [body(): lax.all_to_all(jnp.stack([col_factor] * lax.axis_size('row')), 'row', 0, 0)]
    all_to_all x0 -> x1, waiting for transfers between devices: none -> 4.08 us  [body(): lax.all_to_all(jnp.stack([col_factor] * lax.axis_size('row')), 'row', 0, 0)]
    reduce_sum x1, other arithmetic: 4.59 us -> 1.22 us  [reduce_inner(): pieces.append(jnp.sum(block * row_panel[None, :, :], axis=1))]
    unnamed x15 -> x9, local copies, waits for them, and re-layouts: 3.83 us -> 1.27 us
    unnamed x1, blocking collectives: 37.1 us -> 35.2 us
    another operation x0 -> x1, local copies, waits for them, and re-layouts: none -> 1.48 us  [body(): jnp.stack([col_factor] * lax.axis_size('row'))]
  transfers between devices with their start and end apart: 1 -> 2, of which waited for: 0 -> 1; matrix products, arithmetic and copies ran while one was open for 5% -> 2% of each run, Pallas kernels for 0% -> 0%
where the time goes in v1:
time: 88.4 us; the launch traced here: 88 us
  blocking collectives  40.3 us (46%)
  matrix products  14.9 us (17%)
  between operations  14.8 us (17%)
  starting transfers between devices  7.32 us (8%)
  local copies, waits for them, and re-layouts  4.13 us (5%)
  waiting for transfers between devices  4.1 us (5%)
  other arithmetic  2.56 us (3%)
    unnamed x1, blocking collectives  35.2 us
    dot_general x1, matrix products, body(): inner = jnp.dot(flat, columns, preferred_element_type=jnp.float32)  14.9 us
    all_to_all x1, starting transfers between devices, body(): lax.all_to_all(jnp.stack([col_factor] * lax.axis_size('row')), 'row', 0, 0)  7.28 us
    all_to_all x1, waiting for transfers between devices, body(): lax.all_to_all(jnp.stack([col_factor] * lax.axis_size('row')), 'row', 0, 0)  4.08 us
    psum x1, blocking collectives, body(): aux_result = lax.psum(scattered, 'col')  3.04 us
    all_gather x1, blocking collectives, body(): lax.all_gather(row_factor, 'col', axis=0, tiled=True).astype(jnp.float32)  2.07 us
  transfers between devices with their start and end apart: 2, of which 1 were waited for; matrix products, arithmetic and copies ran while one was open for 2% of the time, Pallas kernels for 0%

profile of v1, /device:TPU:0, one launch (start us, length us, event | category | flops | bytes accessed | tf_op | source)
XLA Modules:
  0.0 88.0 jit_solution(16200072867826063831)
XLA Ops:
  7.2 1.5 %stack.2 = bf16[8,128,128]{2,1,0:T(8,128)(2,1)} broadcast(bf16[128,128]{1,0:T(8,128)(2,1)} %param.7), dimensions={1,2} | broadcast | bytes 294912 | tf_op jit(solution)/shard_map/stack | solution.py:26
  8.6 7.3 %all-to-all-start = ((bf16[8,128,128]{2,1,0:T(8,128)(2,1)}), bf16[8,128,128]{2,1,0:T(8,128)(2,1)S(1)}, u32[]{:S(2)}, u32[]{:S(2)}) async-start(bf16[8,128,128]{2,1,0:T(8,128)(2,1)} %stack.2), calls=%async_computation | async-start | bytes 524288 | tf_op jit(solution)/shard_map/all_to_all | solution.py:26
  15.9 0.0 reduce-scatter.2.cloned.1.call-start
  16.0 2.1 %all_gather.3 = bf16[256,128]{1,0:T(8,128)(2,1)S(1)} all-gather(bf16[128,128]{1,0:T(8,128)(2,1)} %param.6), channel_id=1, replica_groups=mesh['row'=8,'col'=2,'rank'=2] {'col'}, dimensions={0}, use_global_device_ids=true | all-gather | bytes 98304 | tf_op jit(solution)/shard_map/all_gather | solution.py:20
  18.1 1.2 %dynamic-slice = u32[1]{0:T(128)} dynamic-slice(u32[32]{0:T(128)} %constant.4, u32[]{:T(128)S(6)} %add.35), dynamic_slice_sizes={1} | dynamic-slice | bytes 12
  20.0 0.8 fusion.1
  20.8 4.1 %all-to-all-done = bf16[8,128,128]{2,1,0:T(8,128)(2,1)S(1)} async-done(((bf16[8,128,128]{2,1,0:T(8,128)(2,1)}), bf16[8,128,128]{2,1,0:T(8,128)(2,1)S(1)}, u32[]{:S(2)}, u32[]{:S(2)}) %all-to-all-start) | async-done | bytes 262176 | tf_op jit(solution)/shard_map/all_to_all | solution.py:26
  24.8 14.9 %fusion.2 = f32[16384,128]{1,0:T(8,128)S(1)} fusion(bf16[16384,1024]{1,0:T(8,128)(2,1)} %bitcast.21, bf16[1024,128]{1,0:T(8,128)(2,1)S(1)} %bitcast.30), kind=kOutput, calls=%fused_computation.28 | convolution fusion | flops 4294967296 | bytes 42205184 | tf_op jit(solution)/shard_map/dot_general | solution.py:28
  39.7 0.6 fusion
  40.3 1.2 %multiply_reduce_fusion = (f32[8,128]{1,0:T(8,128)S(1)}, f32[8,128]{1,0:T(8,128)S(1)}, f32[8,128]{1,0:T(8,128)S(1)}, f32[8,128]{1,0:T(8,128)S(1)}, f32[8,128]{1,...) fusion(f32[256,128]{1,0:T(8,128)S(1)} %convert_element_type.7, ...), kind=kLoop, calls=%fused_computation | loop fusion | flops 4186112 | bytes 8552448 | tf_op jit(solution)/shard_map/reduce_sum | solution.py:15
  41.5 0.2 multiply_reduce_fusion.14
  41.7 0.2 multiply_reduce_fusion.8
  41.9 0.2 multiply_reduce_fusion.10
  42.0 0.2 multiply_reduce_fusion.12
  42.2 0.7 add_add_fusion
  42.9 0.0 reduce-scatter.2.cloned.1.call-update
  43.0 35.2 %all-reduce = f32[64,128]{1,0:T(8,128)S(1)} all-reduce(f32[64,128]{1,0:T(8,128)S(1)} %constant_dynamic-update-slice_fusion), channel_id=3, replica_groups=mesh['row'=8,'col'=2,'rank'=2] {'row'}, use_global_device_ids=true, to_apply=%region_17.0.clone | all-reduce | flops 8192 | bytes 65536
  78.1 3.0 %psum.7 = f32[8,128]{1,0:T(8,128)} all-reduce(f32[8,128]{1,0:T(8,128)S(1)} %constant_dynamic-slice_fusion), channel_id=1, replica_groups=mesh['row'=8,'col'=2,'rank'=2] {'col'}, use_global_device_ids=true, to_apply=%region_18.0 | all-reduce | flops 1024 | bytes 8192 | tf_op jit(solution)/shard_map/psum | solution.py:33
  81.2 0.0 reduce-scatter.2.cloned.1.call-done
  (10 shorter events, 0.0 us)
Async XLA Ops:
  8.6 16.2 %all-to-all-start = ((bf16[8,128,128]{2,1,0:T(8,128)(2,1)}), bf16[8,128,128]{2,1,0:T(8,128)(2,1)S(1)}, u32[]{:S(2)}, u32[]{:S(2)}) async-start(bf16[8,128,128]{2,1,0:T(8,128)(2,1)} %stack.2), calls=%async_computation | async-start | bytes 524288 | tf_op jit(solution)/shard_map/all_to_all | solution.py:26
  15.9 65.2 %reduce-scatter.2.cloned.1.call-start = ((), (), s32[]{:S(2)}) async-start(), calls=%async_computation.2 | async-start | bytes 196608 | tf_op jit(solution)/shard_map/reduce_scatter | solution.py:31
Sparse Core Ops, SparseCore 0:
  43.0 6.5 reduce-scatter.1
